TPU v7x, 32 devices: a whole 2x2x4 slice. The times are simulated.
32 devices in a mesh: grp: 2 (over y), col: 8 (over z, x), row: 2 (over core).
Axes of the slice: x: 2, y: 2, z: 4, core: 2. Of those that a mesh axis runs over, the one named last changes fastest.
Arguments:
- left_bounds: bfloat16 [4, 8, 128, 8, 128], P(('grp', 'row'), 'col'), parts along dimension 0, may hold values from -0.1875 to 0.1875
- right_bounds: bfloat16 [4, 8, 128, 8, 128], P(('grp', 'row'), 'col'), parts along dimension 0, may hold values from -0.1875 to 0.1875
- site_tensors: bfloat16 [4, 8, 2, 4096], P(('grp', 'row'), 'col'), parts along dimension 0, may hold values from -2 to 2
- configuration: int32 [4, 8], P(('grp', 'row'), 'col'), parts along dimension 0, may hold values from 0 to 1
- top_env: bfloat16 [16, 128, 8, 128], P(('grp', 'col')), parts along dimension 0, may hold values from -6 to 6
- bottom_env: bfloat16 [16, 128, 8, 128], P(('grp', 'col')), parts along dimension 0, may hold values from -6 to 6
- sketch: bfloat16 [1024, 128], replicated, may hold values from -0.1875 to 0.1875
Outputs:
- gradient: float32 [4, 8, 2, 4096], P(('grp', 'row'), 'col'), parts along dimension 0
- left_updated: bfloat16 [4, 8, 128, 8, 128], P(('grp', 'row'), 'col'), parts along dimension 0
- right_updated: bfloat16 [4, 8, 128, 8, 128], P(('grp', 'row'), 'col'), parts along dimension 0
There are 2 independent parts, one for each index of `grp`. A program takes and returns all parts, laid end to end along the dimension named above; an argument that names none is the same for every part. Nothing has to cross between parts.
All inputs are finite; a program needn't handle non-finite values.
Results may differ from a plain program's by a relative error of at most 0.015.
Values may be sent and summed in bfloat16 or wider, within the bound.
A program may use at most 64 MiB of HBM per device.

v0:
```python
import jax
import jax.numpy as jnp
from jax import lax
from jax.experimental import pallas as pl
from jax.experimental.pallas import tpu as pltpu
from jax.sharding import PartitionSpec as P

HIGHEST = lax.Precision.HIGHEST
BLOCK = 8


def shift(value, axis, distance):
    count = lax.axis_size(axis)
    return lax.ppermute(value, axis, [(i, (i + distance) % count) for i in range(count)])


def shift_down(value, distance):
    count, rows = lax.axis_size("col"), lax.axis_size("row")
    route = [(i * rows, (i + distance) % count * rows + 1) for i in range(count)]
    return lax.ppermute(value, ("col", "row"), route)


def dot(lhs, rhs, dims, precision=None):
    return lax.dot_general(
        lhs, rhs, (dims, ((), ())), precision=precision, preferred_element_type=jnp.float32
    )


def spread_row(value, row):
    return jnp.broadcast_to(value[row : row + 1, :], value.shape)


def eliminate_panel(rows, start):
    size = rows.shape[1] // 2
    shape = (BLOCK, size)
    sublane = lax.broadcasted_iota(jnp.int32, shape, 0)
    turned = pltpu.roll(rows[:, :size], size - start, axis=1)
    columns = [jnp.broadcast_to(turned[:, c : c + 1], shape) for c in range(BLOCK)]
    halves = [rows[:, :size], rows[:, size:]]
    for c in range(BLOCK):
        scale = lax.rsqrt(spread_row(columns[c], c))
        factor = jnp.where(
            sublane > c, columns[c] * (scale * scale), jnp.where(sublane == c, 1.0 - scale, 0.0)
        )
        halves = [value - factor * spread_row(value, c) for value in halves]
        for k in range(c + 1, BLOCK):
            columns[k] = columns[k] - factor * spread_row(columns[k], c)
    return halves


def inverse_factors(grams, state):
    size = grams[0].shape[0]
    ones = (
        lax.broadcasted_iota(jnp.int32, (size, size), 0)
        == lax.broadcasted_iota(jnp.int32, (size, size), 1)
    ).astype(jnp.float32)
    for q, gram in enumerate(grams):
        state[q, :, :size] = gram
        state[q, :, size:] = ones
    lane = lax.broadcasted_iota(jnp.int32, (BLOCK, size), 1)

    def step(i, carry):
        start = pl.multiple_of(i * BLOCK, BLOCK)
        for q in range(len(grams)):
            rows, inverse = eliminate_panel(state[q, pl.ds(start, BLOCK), :], start)
            below = jnp.where(lane >= start + BLOCK, rows, 0.0)
            solved = jnp.concatenate([rows, inverse], axis=1)
            state[q] = state[q] - dot(below, solved, ((0,), (0,)), HIGHEST)
            state[q, pl.ds(start, BLOCK), :] = solved
        return carry

    lax.fori_loop(0, size // BLOCK, step, 0)
    return [state[q, :, size:] for q in range(len(grams))]


def row_block(i, size):
    return pl.ds(pl.multiple_of(i * size, size), size)


def gram_of(source, size):
    precision = HIGHEST if source.dtype == jnp.float32 else None

    def step(i, total):
        block = source[row_block(i, size), :]
        return total + dot(block, block, ((0,), (0,)), precision)

    start = jnp.zeros((size, size), jnp.float32)
    return lax.fori_loop(0, source.shape[0] // size, step, start)


def apply_transposed(source, inverse, out):
    size = inverse.shape[0]
    if source.dtype == jnp.float32:

        def step(i, carry):
            block = dot(source[row_block(i, size), :], inverse, ((1,), (1,)), HIGHEST)
            out[row_block(i, size), :] = block.astype(jnp.bfloat16)
            return carry

    else:
        high = inverse.astype(jnp.bfloat16)
        rest = inverse - high.astype(jnp.float32)
        middle = rest.astype(jnp.bfloat16)
        low = (rest - middle.astype(jnp.float32)).astype(jnp.bfloat16)

        def step(i, carry):
            block = source[row_block(i, size), :]
            total = dot(block, low, ((1,), (1,)))
            total = total + dot(block, middle, ((1,), (1,)))
            total = total + dot(block, high, ((1,), (1,)))
            out[row_block(i, size), :] = total.astype(jnp.bfloat16)
            return carry

    lax.fori_loop(0, source.shape[0] // size, step, 0)


BF16 = jnp.bfloat16
F32 = jnp.float32


def half(value):
    return value.astype(BF16)


def flat(ref):
    outer, inner, lane = ref.shape
    return ref.reshape(outer * inner, lane)


def split_legs(matrix, rows_ref, count):
    size = rows_ref.shape[0] // count
    rows_ref[...] = matrix.astype(jnp.float32)
    return [half(rows_ref[pl.ds(leg, size, stride=count), :]) for leg in range(count)]


def stack(planes, target):
    size = planes[0].shape[0]
    for i, plane in enumerate(planes):
        target[i * size : (i + 1) * size, :] = plane


def project(planes, boundary, target):
    size = planes.shape[1]
    count = planes.shape[0] // size
    rows = flat(target)

    def step(u, carry):
        product = dot(planes[row_block(u, size), :], boundary, ((0,), (0,)))
        for k in range(count):
            rows[pl.ds(u * count + k, size, stride=count * count), :] = product[
                :, k * size : (k + 1) * size
            ]
        return carry

    lax.fori_loop(0, count, step, 0)


def pair_up(matrix, others, swap, target):
    outer, inner, lane = target.shape
    bond = matrix.shape[0] // outer
    dims = ((1,), (1,)) if swap else ((1,), (0,))
    left = matrix[...]

    def step(d, carry):
        product = dot(left, others[row_block(d, lane), :], dims)
        target[:, row_block(d, bond), :] = product.reshape(outer, bond, lane)
        return carry

    lax.fori_loop(0, bond, step, 0)


def mix(weights, source, store):
    outer, inner, lane = source.shape
    rows = flat(source)
    group = 8

    def step(i, carry):
        blocks = []
        for j in range(group):
            begin = pl.multiple_of((i * group + j) * inner, inner)
            blocks.append(half(rows[pl.ds(begin, inner), :]))
        product = dot(weights, jnp.concatenate(blocks, axis=1), ((1,), (0,)))
        for j in range(group):
            store(i * group + j, product[:, j * lane : (j + 1) * lane])
        return carry

    lax.fori_loop(0, outer // group, step, 0)


def store_natural(target):
    inner = target.shape[1]
    rows = flat(target)

    def store(index, block):
        rows[pl.ds(pl.multiple_of(index * inner, inner), inner), :] = block

    return store


def store_by_leg(target, bond):
    length = target.shape[0] * bond
    rows = flat(target)

    def store(index, block):
        for d in range(bond):
            begin = pl.multiple_of(d * length + index * bond, bond)
            rows[pl.ds(begin, bond), :] = block[d * bond : (d + 1) * bond]

    return store


def leg_block(source, d, bond):
    length = source.shape[0] * bond
    return half(flat(source)[row_block(d, length), :])


def joined(planes):
    return jnp.concatenate(planes, axis=1)


def edge_kernel(env_ref, left_out, right_out, rows_ref, left_ref, right_ref, state_ref):
    size = env_ref.shape[1]
    planes = split_legs(env_ref[...], rows_ref, env_ref.shape[0] // size)
    stack(planes, left_ref)
    stack([plane.T for plane in planes], right_ref)
    inverses = inverse_factors([gram_of(left_ref, size), gram_of(right_ref, size)], state_ref)
    apply_transposed(left_ref, inverses[0], left_out)
    apply_transposed(right_ref, inverses[1], right_out)


def upper_kernel(
    left_base, right_base, west_ref, east_ref, left_mix, right_mix, sketch_ref,
    left_next, right_next, left_bulk, right_bulk,
    rows_ref, part_ref, absorbed_ref, left_sum, right_sum, state_ref,
):
    size = west_ref.shape[1]
    bond = west_ref.shape[0] // size
    for base, boundary, weights, bulk, total in (
        (left_base, west_ref, left_mix, left_bulk, left_sum),
        (right_base, east_ref, right_mix, right_bulk, right_sum),
    ):
        project(base, joined(split_legs(boundary[...], rows_ref, bond)), part_ref)
        mix(weights[...], part_ref, store_by_leg(absorbed_ref, bond))

        def step(d, carry, bulk=bulk, total=total):
            block = leg_block(absorbed_ref, d, bond)
            bulk[d] = block
            total[row_block(d, size), :] = dot(block, sketch_ref[...], ((0,), (0,)))
            return carry

        lax.fori_loop(0, bond, step, 0)
    inverses = inverse_factors([gram_of(left_sum, size), gram_of(right_sum, size)], state_ref)
    apply_transposed(left_sum, inverses[0], left_next)
    apply_transposed(right_sum, inverses[1], right_next)


def lower_kernel(
    left_edge, right_edge, west_ref, east_ref, left_mix, right_mix,
    top_ref, bottom_ref, west_above, east_above, down_mix,
    left_bulk, right_bulk, grad_above, grad_here,
    rows_ref, first_ref, second_ref, third_ref, mixed_ref, state_ref,
):
    size = west_ref.shape[1]
    bond = west_ref.shape[0] // size
    steps = bond * bond
    for edge, boundary, weights, bulk in (
        (left_edge, west_ref, left_mix, left_bulk),
        (right_edge, east_ref, right_mix, right_bulk),
    ):
        pair_up(boundary, edge, False, first_ref)
        mix(weights[...], first_ref, store_natural(mixed_ref))

        def step(o, carry, bulk=bulk):
            for u in range(bond):
                bulk[o, u * size : (u + 1) * size, :] = half(
                    flat(mixed_ref)[pl.ds(u * bond + o, size, stride=steps), :]
                )
            return carry

        lax.fori_loop(0, bond, step, 0)
    west_0 = joined(split_legs(west_above[...], rows_ref, bond))
    west_1 = joined(split_legs(west_ref[...], rows_ref, bond))
    stack(split_legs(top_ref[...], rows_ref, bond), state_ref)
    project(state_ref, west_0, first_ref)
    mix(down_mix[...], first_ref, store_by_leg(mixed_ref, bond))

    def down(d, carry):
        block = leg_block(mixed_ref, d, bond)
        state_ref[row_block(d, size), :] = half(dot(block, east_above[...], ((0,), (0,))))
        return carry

    lax.fori_loop(0, bond, down, 0)
    project(state_ref, west_1, third_ref)
    stack(split_legs(bottom_ref[...], rows_ref, bond), state_ref)
    pair_up(east_ref, state_ref, True, second_ref)
    mix(right_mix[...], second_ref, store_natural(mixed_ref))
    overlap(third_ref, second_ref, grad_here)

    def up(u, carry):
        low = joined(
            [
                half(flat(mixed_ref)[pl.ds(u * bond + k, size, stride=steps), :])
                for k in range(bond)
            ]
        )
        state_ref[row_block(u, size), :] = half(dot(west_1, low, ((1,), (1,))))
        return carry

    lax.fori_loop(0, bond, up, 0)
    pair_up(east_above, state_ref, True, second_ref)
    overlap(first_ref, second_ref, grad_above)


def overlap(part_ref, key_ref, out_ref):
    outer, inner, lane = part_ref.shape
    group = 8

    def gather(ref, i):
        rows = flat(ref)
        return joined(
            [
                half(rows[pl.ds(pl.multiple_of((i * group + j) * inner, inner), inner), :])
                for j in range(group)
            ]
        )

    def step(i, total):
        return total + dot(gather(part_ref, i), gather(key_ref, i), ((1,), (1,)))

    out_ref[...] = lax.fori_loop(
        0, outer // group, step, jnp.zeros((inner, inner), jnp.float32)
    )


def upper_end_kernel(
    left_bulk, right_bulk, left_basis, right_basis, left_out, right_out, rows_ref
):
    for bulk, basis, out in (
        (left_bulk, left_basis, left_out),
        (right_bulk, right_basis, right_out),
    ):
        bond, length, size = bulk.shape

        def step(i, total, bulk=bulk, basis=basis):
            rows = row_block(i, size)
            block = dot(
                joined([bulk[d, rows, :] for d in range(bond)]), basis[...], ((1,), (0,))
            )
            rows_ref[rows, :] = block
            return total + jnp.sum(block * block, axis=0, keepdims=True)

        scaled_out(lax.fori_loop(0, length // size, step, jnp.zeros((1, size))), rows_ref, out)


def scaled_out(total, rows_ref, out):
    mean = jnp.sum(total, keepdims=True) * (1.0 / (rows_ref.shape[0] * rows_ref.shape[1]))
    out[...] = half(rows_ref[...] * lax.rsqrt(mean + 1e-06))


def lower_end_kernel(
    left_bulk, right_bulk, left_basis, right_basis, left_out, right_out, rows_ref
):
    for bulk, basis, out in (
        (left_bulk, left_basis, left_out),
        (right_bulk, right_basis, right_out),
    ):
        bond, length, size = bulk.shape
        flipped = basis[...].T

        def step(o, total, bulk=bulk, flipped=flipped):
            block = dot(flipped, bulk[o], ((1,), (0,)))
            rows_ref[pl.ds(o, size, stride=bond), :] = block
            return total + jnp.sum(block * block, axis=0, keepdims=True)

        scaled_out(lax.fori_loop(0, bond, step, jnp.zeros((1, size))), rows_ref, out)


def run(kernel, outs, scratch, flops, *args):
    in_vmem = pl.BlockSpec(memory_space=pltpu.VMEM)
    return pl.pallas_call(
        kernel,
        out_shape=tuple(jax.ShapeDtypeStruct(shape, kind) for shape, kind in outs),
        in_specs=[in_vmem] * len(args),
        out_specs=(in_vmem,) * len(outs),
        scratch_shapes=[pltpu.VMEM(shape, kind) for shape, kind in scratch],
        compiler_params=pltpu.CompilerParams(vmem_limit_bytes=48 * 1024 * 1024),
        cost_estimate=pl.CostEstimate(
            flops=flops, bytes_accessed=2_000_000, transcendentals=0
        ),
    )(*args)


def local(left_bounds, right_bounds, site_tensors, configuration, top_env, bottom_env, sketch):
    chi = left_bounds.shape[2]
    bond = left_bounds.shape[3]
    phys = site_tensors.shape[2]
    tall = (chi * bond, chi)
    wide = (bond, chi * bond, chi)
    pair = (2, chi, 2 * chi)
    square = (bond * bond, bond * bond)
    volume = (chi, bond * bond, chi)
    row = lax.axis_index("row")
    leading = row == 0
    left_flat = left_bounds.reshape(tall)
    right_flat = right_bounds.reshape(tall)
    western = shift(left_flat, "col", 1)
    eastern = shift(right_flat, "col", -1)
    western_0 = shift_down(left_flat, 1)
    eastern_0 = shift_down(right_flat, -1)
    selection = (
        lax.broadcasted_iota(jnp.int32, (1, 1, phys, 1), 2) == configuration[:, :, None, None]
    )
    selected = jnp.sum(jnp.where(selection, site_tensors, jnp.zeros_like(site_tensors)), axis=2)
    core = selected.reshape(bond, bond, bond, bond)
    core_0 = lax.ppermute(selected.reshape(-1), "row", [(0, 1)]).reshape(core.shape)
    env = jnp.where(leading, top_env[0], bottom_env[0]).reshape(tall)
    base_left, base_right = run(
        edge_kernel,
        [(tall, BF16)] * 2,
        [(tall, F32), (tall, BF16), (tall, BF16), (pair, F32)],
        10_000_000_000,
        env,
    )

    def upper():
        next_left, next_right, bulk_left, bulk_right = run(
            upper_kernel,
            [(tall, BF16)] * 2 + [(wide, BF16)] * 2,
            [(tall, F32), (volume, F32), (volume, F32), (tall, F32), (tall, F32), (pair, F32)],
            10_000_000_000,
            base_left,
            base_right,
            western,
            eastern,
            core.transpose(3, 2, 1, 0).reshape(square),
            core.transpose(3, 0, 1, 2).reshape(square),
            sketch,
        )
        blank = jnp.zeros(square, jnp.float32)
        return next_left, next_right, bulk_left, bulk_right, blank, blank

    def lower():
        bulk_left, bulk_right, grad_0, grad_1 = run(
            lower_kernel,
            [(wide, BF16)] * 2 + [(square, jnp.float32)] * 2,
            [(tall, F32)] + [(volume, F32)] * 4 + [(tall, BF16)],
            10_000_000_000,
            base_left,
            base_right,
            western,
            eastern,
            core.transpose(1, 2, 3, 0).reshape(square),
            core.transpose(1, 0, 3, 2).reshape(square),
            top_env.reshape(tall),
            bottom_env.reshape(tall),
            western_0,
            eastern_0,
            core_0.transpose(3, 2, 1, 0).reshape(square),
        )
        blank = jnp.zeros(tall, BF16)
        return blank, blank, bulk_left, bulk_right, grad_0, grad_1

    next_left, next_right, bulk_left, bulk_right, grad_0, grad_1 = lax.cond(
        leading, upper, lower
    )
    sent_left = lax.ppermute(next_left, "row", [(0, 1)])
    sent_right = lax.ppermute(next_right, "row", [(0, 1)])
    grad_sent = lax.ppermute(grad_0, "row", [(1, 0)])

    def upper_end():
        return run(
            upper_end_kernel, [(tall, BF16)] * 2, [(tall, F32)], 1_000_000_000,
            bulk_left, bulk_right, next_left, next_right,
        )

    def lower_end():
        return run(
            lower_end_kernel, [(tall, BF16)] * 2, [(tall, F32)], 1_000_000_000,
            bulk_left, bulk_right, sent_left, sent_right,
        )

    left_new, right_new = lax.cond(leading, upper_end, lower_end)
    gradient = jnp.where(leading, grad_sent, grad_1).reshape(bond, bond, bond, bond)
    gradient = gradient.transpose(1, 0, 3, 2).reshape(1, 1, 1, bond**4)
    gradient = jnp.where(selection, gradient * (bond / chi), 0.0)
    return (
        gradient,
        left_new.reshape(left_bounds.shape),
        right_new.reshape(right_bounds.shape),
    )


def solution(mesh):
    return jax.shard_map(
        local,
        mesh=mesh,
        in_specs=(
            P(("grp", "row"), "col", None, None, None),
            P(("grp", "row"), "col", None, None, None),
            P(("grp", "row"), "col", None, None),
            P(("grp", "row"), "col"),
            P(("grp", "col"), None, None, None),
            P(("grp", "col"), None, None, None),
            P(),
        ),
        out_specs=(
            P(("grp", "row"), "col", None, None),
            P(("grp", "row"), "col", None, None, None),
            P(("grp", "row"), "col", None, None, None),
        ),
        check_vma=False,
    )
```

profile of v0, /device:TPU:0, one launch (start us, length us, event | category | flops | bytes accessed | tf_op | source)
XLA Modules:
  0.0 107.2 jit_solution(9834014800153444866)
XLA Ops:
  0.6 4.3 %collective-permute-start.3 = (bf16[1024,128]{1,0:T(8,128)(2,1)}, bf16[1024,128]{1,0:T(8,128)(2,1)S(1)}, u32[]{:S(2)}, u32[]{:S(2)}) collective-permute-start(bf16[1024,128]{1,0:T(8,128)(2,1)} %bitcast.40), channel_id=1, source_target_pairs={{0,3},{2,5},{4,7},{6,9},{8,11},{10,13},{12,15},{14,1},{16,19},{18,... | collective-permute-start | bytes 786440 | tf_op jit(solution)/shard_map/ppermute | solution.py:20
  4.9 1.6 %collective-permute-start.1 = (bf16[1024,128]{1,0:T(8,128)(2,1)}, bf16[1024,128]{1,0:T(8,128)(2,1)S(1)}, u32[]{:S(2)}, u32[]{:S(2)}) collective-permute-start(bf16[1024,128]{1,0:T(8,128)(2,1)} %bitcast.41), channel_id=1, source_target_pairs={{0,2},{2,4},{4,6},{6,8},{8,10},{10,12},{12,14},{14,0},{1,3},{3,5},... | collective-permute-start | bytes 786440 | tf_op jit(solution)/shard_map/ppermute | solution.py:14
  6.5 2.8 %collective-permute-start.4 = (bf16[1024,128]{1,0:T(8,128)(2,1)}, bf16[1024,128]{1,0:T(8,128)(2,1)S(1)}, u32[]{:S(2)}, u32[]{:S(2)}) collective-permute-start(bf16[1024,128]{1,0:T(8,128)(2,1)} %bitcast.42), channel_id=1, source_target_pairs={{0,15},{2,1},{4,3},{6,5},{8,7},{10,9},{12,11},{14,13},{16,31},{18,... | collective-permute-start | bytes 786440 | tf_op jit(solution)/shard_map/ppermute | solution.py:20
  9.3 1.8 %collective-permute-start.2 = (bf16[1024,128]{1,0:T(8,128)(2,1)}, bf16[1024,128]{1,0:T(8,128)(2,1)S(1)}, u32[]{:S(2)}, u32[]{:S(2)}) collective-permute-start(bf16[1024,128]{1,0:T(8,128)(2,1)} %bitcast.43), channel_id=1, source_target_pairs={{0,14},{2,0},{4,2},{6,4},{8,6},{10,8},{12,10},{14,12},{1,15},{3,1}... | collective-permute-start | bytes 786440 | tf_op jit(solution)/shard_map/ppermute | solution.py:14
  11.8 0.8 fusion
  12.6 1.3 %collective-permute-start = (bf16[4096]{0:T(1024)(128)(2,1)S(1)}, bf16[4096]{0:T(1024)(128)(2,1)S(1)}, u32[]{:S(2)}, u32[]{:S(2)}) collective-permute-start(bf16[4096]{0:T(1024)(128)(2,1)S(1)} %fusion), channel_id=1, source_target_pairs={{0,1},{2,3},{4,5},{6,7},{8,9},{10,11},{12,13},{14,15},{16,17},{18,... | collective-permute-start | bytes 24584 | tf_op jit(solution)/shard_map/ppermute | solution.py:415
  13.9 1.0 select_bitcast_fusion.env_ref
  14.9 27.7 %shard_map.95 = (bf16[1024,128]{1,0:T(8,128)(2,1)}, bf16[1024,128]{1,0:T(8,128)(2,1)}) custom-call(bf16[1024,128]{1,0:T(8,128)(2,1)S(1)} %select_bitcast_fusion.env_ref), custom_call_target="tpu_custom_call" | custom-call | flops 10000000000 | bytes 2000000 | tf_op jit(solution)/shard_map/pallas_call | solution.py:380
  42.6 0.2 reshape.132
  42.9 49.8 %conditional.2 = (bf16[1024,128]{1,0:T(8,128)(2,1)S(1)}, bf16[1024,128]{1,0:T(8,128)(2,1)S(1)}, bf16[8,1024,128]{2,1,0:T(8,128)(2,1)S(1)}, bf16[8,1024,128]{2,1,...) conditional(s32[]{:T(128)} %convert_element_type.2, (bf16[8,8,8,8]{3,2,1,0:T(8,128)(2,1)S(1)}, ...), branch_computations={%region_1.2_spmd, %region_2.3_spmd} | conditional | flops 10000000000 | bytes 4736236 | solution.py:463
  42.9 0.3 copy.16
  43.3 0.1 reshape.123.left_mix
  43.4 0.3 copy.18
  43.7 0.1 reshape.124.right_mix
  43.8 48.8 %branch_1_fun.2 = (bf16[1024,128]{1,0:T(8,128)(2,1)S(1)}, bf16[1024,128]{1,0:T(8,128)(2,1)S(1)}, bf16[8,1024,128]{2,1,0:T(8,128)(2,1)S(1)}, bf16[8,1024,128]{2,1,0:T(8,128)(2,1)}) custom-call(bf16[1024,128]{1,0:T(8,128)(2,1)} %get-tuple-element.69.left_base, bf16[1024,128]{1,0:T(8,128)(2,1)} %get-tuple-element.70.right_base, ...), custom_call_target="tpu_custom_call" | custom-call | flops 10000000000 | bytes 2000000 | tf_op jit(solution)/shard_map/cond/branch_1_fun/pallas_call | solution.py:380
  92.7 1.3 %collective-permute-start.5 = (f32[64,64]{1,0:T(8,128)S(1)}, f32[64,64]{1,0:T(8,128)S(1)}, u32[]{:S(2)}, u32[]{:S(2)}) collective-permute-start(f32[64,64]{1,0:T(8,128)S(1)} %get-tuple-element.106), channel_id=1, source_target_pairs={{1,0},{3,2},{5,4},{7,6},{9,8},{11,10},{13,12},{15,14},{17,16},{19,... | collective-permute-start | bytes 49160 | tf_op jit(solution)/shard_map/ppermute | solution.py:468
  94.0 3.7 %collective-permute-start.6 = (bf16[1024,128]{1,0:T(8,128)(2,1)S(1)}, bf16[1024,128]{1,0:T(8,128)(2,1)}, u32[]{:S(2)}, u32[]{:S(2)}) collective-permute-start(bf16[1024,128]{1,0:T(8,128)(2,1)S(1)} %get-tuple-element.110), channel_id=1, source_target_pairs={{0,1},{2,3},{4,5},{6,7},{8,9},{10,11},{12,13},{14,15},{16,17},{18,... | collective-permute-start | bytes 786440 | tf_op jit(solution)/shard_map/ppermute | solution.py:466
  97.7 2.0 %collective-permute-start.7 = (bf16[1024,128]{1,0:T(8,128)(2,1)S(1)}, bf16[1024,128]{1,0:T(8,128)(2,1)}, u32[]{:S(2)}, u32[]{:S(2)}) collective-permute-start(bf16[1024,128]{1,0:T(8,128)(2,1)S(1)} %get-tuple-element.111), channel_id=1, source_target_pairs={{0,1},{2,3},{4,5},{6,7},{8,9},{10,11},{12,13},{14,15},{16,17},{18,... | collective-permute-start | bytes 786440 | tf_op jit(solution)/shard_map/ppermute | solution.py:467
  99.7 0.1 mul.22
  99.8 0.1 copy.19
  100.0 0.1 mul.24
  100.1 0.7 broadcast_select_fusion
  100.8 6.4 %conditional.3 = (bf16[1,1,128,8,128]{4,3,2,1,0:T(8,128)(2,1)}, bf16[1,1,128,8,128]{4,3,2,1,0:T(8,128)(2,1)}) conditional(s32[]{:T(128)} %convert_element_type.2, (bf16[8,1024,128]{2,1,0:T(8,128)(2,1)S(1)}, bf16[8,1024,128]{2,1,0:T(8,128)(2,1)}, bf16[1024,128]{1,0:T(8,128)(2,1)}, bf16[1024,128]{1,0:T(8,128)(2,1)}) %tuple.30, ...), branch_computations={%region_3.4_spmd, %region_4.5_spmd} | conditional | flops 1000000000 | bytes 2000016 | solution.py:482
  100.8 6.4 %branch_1_fun.3 = (bf16[1024,128]{1,0:T(8,128)(2,1)}, bf16[1024,128]{1,0:T(8,128)(2,1)}) custom-call(bf16[8,1024,128]{2,1,0:T(8,128)(2,1)S(1)} %get-tuple-element.85.left_bulk, bf16[8,1024,128]{2,1,0:T(8,128)(2,1)} %get-tuple-element.86.right_bulk, bf16[1024,128]{1,0:T(8,128)(2,1)S(1)} %get-tuple-element.87.left_basis, ...), custom_call_target="tpu_custom_call" | custom-call | flops 1000000000 | bytes 2000000 | tf_op jit(solution)/shard_map/cond/branch_1_fun/pallas_call | solution.py:380
  (20 shorter events, 0.1 us)
Async XLA Ops:
  0.6 42.2 %collective-permute-start.3 = (bf16[1024,128]{1,0:T(8,128)(2,1)}, bf16[1024,128]{1,0:T(8,128)(2,1)S(1)}, u32[]{:S(2)}, u32[]{:S(2)}) collective-permute-start(bf16[1024,128]{1,0:T(8,128)(2,1)} %bitcast.40), channel_id=1, source_target_pairs={{0,3},{2,5},{4,7},{6,9},{8,11},{10,13},{12,15},{14,1},{16,19},{18,... | collective-permute-start | bytes 786440 | tf_op jit(solution)/shard_map/ppermute | solution.py:20
  4.9 37.9 %collective-permute-start.1 = (bf16[1024,128]{1,0:T(8,128)(2,1)}, bf16[1024,128]{1,0:T(8,128)(2,1)S(1)}, u32[]{:S(2)}, u32[]{:S(2)}) collective-permute-start(bf16[1024,128]{1,0:T(8,128)(2,1)} %bitcast.41), channel_id=1, source_target_pairs={{0,2},{2,4},{4,6},{6,8},{8,10},{10,12},{12,14},{14,0},{1,3},{3,5},... | collective-permute-start | bytes 786440 | tf_op jit(solution)/shard_map/ppermute | solution.py:14
  6.5 36.3 %collective-permute-start.4 = (bf16[1024,128]{1,0:T(8,128)(2,1)}, bf16[1024,128]{1,0:T(8,128)(2,1)S(1)}, u32[]{:S(2)}, u32[]{:S(2)}) collective-permute-start(bf16[1024,128]{1,0:T(8,128)(2,1)} %bitcast.42), channel_id=1, source_target_pairs={{0,15},{2,1},{4,3},{6,5},{8,7},{10,9},{12,11},{14,13},{16,31},{18,... | collective-permute-start | bytes 786440 | tf_op jit(solution)/shard_map/ppermute | solution.py:20
  9.3 33.5 %collective-permute-start.2 = (bf16[1024,128]{1,0:T(8,128)(2,1)}, bf16[1024,128]{1,0:T(8,128)(2,1)S(1)}, u32[]{:S(2)}, u32[]{:S(2)}) collective-permute-start(bf16[1024,128]{1,0:T(8,128)(2,1)} %bitcast.43), channel_id=1, source_target_pairs={{0,14},{2,0},{4,2},{6,4},{8,6},{10,8},{12,10},{14,12},{1,15},{3,1}... | collective-permute-start | bytes 786440 | tf_op jit(solution)/shard_map/ppermute | solution.py:14
  12.6 30.2 %collective-permute-start = (bf16[4096]{0:T(1024)(128)(2,1)S(1)}, bf16[4096]{0:T(1024)(128)(2,1)S(1)}, u32[]{:S(2)}, u32[]{:S(2)}) collective-permute-start(bf16[4096]{0:T(1024)(128)(2,1)S(1)} %fusion), channel_id=1, source_target_pairs={{0,1},{2,3},{4,5},{6,7},{8,9},{10,11},{12,13},{14,15},{16,17},{18,... | collective-permute-start | bytes 24584 | tf_op jit(solution)/shard_map/ppermute | solution.py:415
  14.9 28.0 %copy-start = (bf16[1,128,8,128]{3,2,1,0:T(8,128)(2,1)S(1)}, bf16[1,128,8,128]{3,2,1,0:T(8,128)(2,1)}, u32[]{:S(2)}) copy-start(bf16[1,128,8,128]{3,2,1,0:T(8,128)(2,1)} %param.15) | copy-start | bytes 786436
  14.9 27.9 %copy-start.1 = (bf16[1,128,8,128]{3,2,1,0:T(8,128)(2,1)S(1)}, bf16[1,128,8,128]{3,2,1,0:T(8,128)(2,1)}, u32[]{:S(2)}) copy-start(bf16[1,128,8,128]{3,2,1,0:T(8,128)(2,1)} %param.16) | copy-start | bytes 786436
  14.9 27.9 %copy-start.2 = (bf16[1024,128]{1,0:T(8,128)(2,1)S(1)}, bf16[1024,128]{1,0:T(8,128)(2,1)}, u32[]{:S(2)}) copy-start(bf16[1024,128]{1,0:T(8,128)(2,1)} %param.17) | copy-start | bytes 786436
  42.9 0.8 copy-start.5
  92.7 7.0 %collective-permute-start.5 = (f32[64,64]{1,0:T(8,128)S(1)}, f32[64,64]{1,0:T(8,128)S(1)}, u32[]{:S(2)}, u32[]{:S(2)}) collective-permute-start(f32[64,64]{1,0:T(8,128)S(1)} %get-tuple-element.106), channel_id=1, source_target_pairs={{1,0},{3,2},{5,4},{7,6},{9,8},{11,10},{13,12},{15,14},{17,16},{19,... | collective-permute-start | bytes 49160 | tf_op jit(solution)/shard_map/ppermute | solution.py:468
  94.0 6.9 %collective-permute-start.6 = (bf16[1024,128]{1,0:T(8,128)(2,1)S(1)}, bf16[1024,128]{1,0:T(8,128)(2,1)}, u32[]{:S(2)}, u32[]{:S(2)}) collective-permute-start(bf16[1024,128]{1,0:T(8,128)(2,1)S(1)} %get-tuple-element.110), channel_id=1, source_target_pairs={{0,1},{2,3},{4,5},{6,7},{8,9},{10,11},{12,13},{14,15},{16,17},{18,... | collective-permute-start | bytes 786440 | tf_op jit(solution)/shard_map/ppermute | solution.py:466
  97.7 3.1 %collective-permute-start.7 = (bf16[1024,128]{1,0:T(8,128)(2,1)S(1)}, bf16[1024,128]{1,0:T(8,128)(2,1)}, u32[]{:S(2)}, u32[]{:S(2)}) collective-permute-start(bf16[1024,128]{1,0:T(8,128)(2,1)S(1)} %get-tuple-element.111), channel_id=1, source_target_pairs={{0,1},{2,3},{4,5},{6,7},{8,9},{10,11},{12,13},{14,15},{16,17},{18,... | collective-permute-start | bytes 786440 | tf_op jit(solution)/shard_map/ppermute | solution.py:467
where the time goes:
time: 108 us; the launch traced here: 107 us
  Pallas kernels  82.9 us (77%)
  starting transfers between devices  18.8 us (17%)
  other arithmetic  2.53 us (2%)
  local copies, waits for them, and re-layouts  1.5 us (1%)
  between operations  1.45 us (1%)
    pallas_call x3, Pallas kernels, run(): pl.pallas_call(kernel, out_shape=tuple((jax.ShapeDtypeStruct(shape, kind)...  82.9 us
    ppermute x2, starting transfers between devices, shift_down(): return lax.ppermute(value, ('col', 'row'), route)  7.09 us
    ppermute x1, starting transfers between devices, local(): sent_left = lax.ppermute(next_left, 'row', [(0, 1)])  3.75 us
    ppermute x2, starting transfers between devices, shift(): lax.ppermute(value, axis, [(i, (i + distance) % count) for i in range(cou...  3.37 us
  transfers between devices with their start and end apart: 8, of which 0 were waited for; matrix products, arithmetic and copies ran while one was open for 3% of the time, Pallas kernels for 26%

commit v1 on v0

v1 whole, which is shorter than its diff:
```python
import jax
import jax.numpy as jnp
from jax import lax
from jax.experimental import pallas as pl
from jax.experimental.pallas import tpu as pltpu
from jax.sharding import PartitionSpec as P

HIGHEST = lax.Precision.HIGHEST
BLOCK = 8


def shift(value, axis, distance):
    count = lax.axis_size(axis)
    return lax.ppermute(value, axis, [(i, (i + distance) % count) for i in range(count)])


def dot(lhs, rhs, dims, precision=None):
    return lax.dot_general(
        lhs, rhs, (dims, ((), ())), precision=precision, preferred_element_type=jnp.float32
    )


def spread_row(value, row):
    return jnp.broadcast_to(value[row : row + 1, :], value.shape)


def eliminate_panel(rows, inverse, start):
    sublane = lax.broadcasted_iota(jnp.int32, rows.shape, 0)
    columns = [
        jnp.broadcast_to(rows[:, start + c : start + c + 1], rows.shape) for c in range(BLOCK)
    ]
    for c in range(BLOCK):
        scale = lax.rsqrt(spread_row(columns[c], c))
        factor = jnp.where(
            sublane > c, columns[c] * (scale * scale), jnp.where(sublane == c, 1.0 - scale, 0.0)
        )
        rows = rows - factor * spread_row(rows, c)
        inverse = inverse - factor * spread_row(inverse, c)
        for k in range(c + 1, BLOCK):
            columns[k] = columns[k] - factor * spread_row(columns[k], c)
    return rows, inverse


def inverse_factors(grams):
    size = grams[0].shape[0]
    ones = (
        lax.broadcasted_iota(jnp.int32, (size, size), 0)
        == lax.broadcasted_iota(jnp.int32, (size, size), 1)
    ).astype(jnp.float32)
    states = [jnp.concatenate([gram, ones], axis=1) for gram in grams]
    found = [[] for _ in grams]
    for start in range(0, size, BLOCK):
        for q in range(len(grams)):
            rows, inverse = eliminate_panel(
                states[q][:BLOCK, :size], states[q][:BLOCK, size:], start
            )
            found[q].append(inverse)
            if start + BLOCK < size:
                update = dot(
                    rows, jnp.concatenate([rows, inverse], axis=1), ((0,), (0,)), HIGHEST
                )
                states[q] = states[q][BLOCK:] - update[start + BLOCK :]
    return [jnp.concatenate(blocks, axis=0) for blocks in found]


def loop(count, step, start=0, unroll=2):
    def several(i, carry):
        for j in range(unroll):
            carry = step(i * unroll + j, carry)
        return carry

    return lax.fori_loop(0, count // unroll, several, start)


def row_block(i, size):
    return pl.ds(pl.multiple_of(i * size, size), size)


def gram_of(source, size):
    precision = HIGHEST if source.dtype == jnp.float32 else None

    def step(i, total):
        block = source[row_block(i, size), :]
        return total + dot(block, block, ((0,), (0,)), precision)

    start = jnp.zeros((size, size), jnp.float32)
    return loop(source.shape[0] // size, step, start)


def apply_transposed(source, inverse, out):
    size = inverse.shape[0]
    if source.dtype == jnp.float32:

        def step(i, carry):
            block = dot(source[row_block(i, size), :], inverse, ((1,), (1,)), HIGHEST)
            out[row_block(i, size), :] = block.astype(jnp.bfloat16)
            return carry

    else:
        high = inverse.astype(jnp.bfloat16)
        rest = inverse - high.astype(jnp.float32)
        middle = rest.astype(jnp.bfloat16)
        low = (rest - middle.astype(jnp.float32)).astype(jnp.bfloat16)

        def step(i, carry):
            block = source[row_block(i, size), :]
            total = dot(block, low, ((1,), (1,)))
            total = total + dot(block, middle, ((1,), (1,)))
            total = total + dot(block, high, ((1,), (1,)))
            out[row_block(i, size), :] = total.astype(jnp.bfloat16)
            return carry

    loop(source.shape[0] // size, step)


BF16 = jnp.bfloat16
F32 = jnp.float32


def half(value):
    return value.astype(BF16)


def flat(ref):
    outer, inner, lane = ref.shape
    return ref.reshape(outer * inner, lane)


def split_legs(matrix, rows_ref, count):
    size = rows_ref.shape[0] // count
    rows_ref[...] = matrix.astype(jnp.float32)
    return [half(rows_ref[pl.ds(leg, size, stride=count), :]) for leg in range(count)]


def stack(planes, target):
    size = planes[0].shape[0]
    for i, plane in enumerate(planes):
        target[i * size : (i + 1) * size, :] = plane


def project(planes, boundary, target):
    size = planes.shape[1]
    count = planes.shape[0] // size
    rows = flat(target)

    def step(u, carry):
        product = dot(planes[row_block(u, size), :], boundary, ((0,), (0,)))
        for k in range(count):
            rows[pl.ds(u * count + k, size, stride=count * count), :] = product[
                :, k * size : (k + 1) * size
            ]
        return carry

    loop(count, step)


def pair_up(matrix, others, swap, target):
    outer, inner, lane = target.shape
    bond = matrix.shape[0] // outer
    dims = ((1,), (1,)) if swap else ((1,), (0,))
    left = matrix[...]

    def step(d, carry):
        product = dot(left, others[row_block(d, lane), :], dims)
        target[:, row_block(d, bond), :] = product.reshape(outer, bond, lane)
        return carry

    loop(bond, step)


def mix(weights, source, store):
    outer, inner, lane = source.shape
    rows = flat(source)
    group = 8

    def step(i, carry):
        blocks = []
        for j in range(group):
            begin = pl.multiple_of((i * group + j) * inner, inner)
            blocks.append(half(rows[pl.ds(begin, inner), :]))
        product = dot(weights, jnp.concatenate(blocks, axis=1), ((1,), (0,)))
        for j in range(group):
            store(i * group + j, product[:, j * lane : (j + 1) * lane])
        return carry

    loop(outer // group, step)


def store_natural(target):
    inner = target.shape[1]
    rows = flat(target)

    def store(index, block):
        rows[pl.ds(pl.multiple_of(index * inner, inner), inner), :] = block

    return store


def store_by_leg(target, bond):
    length = target.shape[0] * bond
    rows = flat(target)

    def store(index, block):
        for d in range(bond):
            begin = pl.multiple_of(d * length + index * bond, bond)
            rows[pl.ds(begin, bond), :] = block[d * bond : (d + 1) * bond]

    return store


def leg_block(source, d, bond):
    length = source.shape[0] * bond
    return half(flat(source)[row_block(d, length), :])


def joined(planes):
    return jnp.concatenate(planes, axis=1)


def edge_kernel(env_ref, left_out, right_out, rows_ref, left_ref, right_ref):
    size = env_ref.shape[1]
    planes = split_legs(env_ref[...], rows_ref, env_ref.shape[0] // size)
    stack(planes, left_ref)
    stack([plane.T for plane in planes], right_ref)
    inverses = inverse_factors([gram_of(left_ref, size), gram_of(right_ref, size)])
    apply_transposed(left_ref, inverses[0], left_out)
    apply_transposed(right_ref, inverses[1], right_out)


def upper_kernel(
    left_base, right_base, west_ref, east_ref, left_mix, right_mix, sketch_ref,
    next_ref, left_bulk, right_bulk, rows_ref, part_ref, absorbed_ref, left_sum, right_sum,
):
    size = west_ref.shape[1]
    bond = west_ref.shape[0] // size
    for base, boundary, weights, bulk, total in (
        (left_base, west_ref, left_mix, left_bulk, left_sum),
        (right_base, east_ref, right_mix, right_bulk, right_sum),
    ):
        project(base, joined(split_legs(boundary[...], rows_ref, bond)), part_ref)
        mix(weights[...], part_ref, store_by_leg(absorbed_ref, bond))

        def step(d, carry, bulk=bulk, total=total):
            block = leg_block(absorbed_ref, d, bond)
            bulk[d] = block
            total[row_block(d, size), :] = dot(block, sketch_ref[...], ((0,), (0,)))
            return carry

        loop(bond, step)
    inverses = inverse_factors([gram_of(left_sum, size), gram_of(right_sum, size)])
    length = left_sum.shape[0]
    apply_transposed(left_sum, inverses[0], next_ref.at[:length])
    apply_transposed(right_sum, inverses[1], next_ref.at[length:])


def lower_kernel(
    left_edge, right_edge, west_ref, east_ref, left_mix, right_mix,
    left_bulk, right_bulk, first_ref, mixed_ref,
):
    size = west_ref.shape[1]
    bond = west_ref.shape[0] // size
    steps = bond * bond
    for edge, boundary, weights, bulk in (
        (left_edge, west_ref, left_mix, left_bulk),
        (right_edge, east_ref, right_mix, right_bulk),
    ):
        pair_up(boundary, edge, False, first_ref)
        mix(weights[...], first_ref, store_natural(mixed_ref))

        def step(o, carry, bulk=bulk):
            for u in range(bond):
                bulk[o, u * size : (u + 1) * size, :] = half(
                    flat(mixed_ref)[pl.ds(u * bond + o, size, stride=steps), :]
                )
            return carry

        loop(bond, step)


def down_kernel(
    env_ref, west_ref, east_ref, weights, kept_ref, state_ref,
    rows_ref, planes_ref, first_ref, mixed_ref,
):
    size = west_ref.shape[1]
    bond = west_ref.shape[0] // size
    west = joined(split_legs(west_ref[...], rows_ref, bond))
    stack(split_legs(env_ref[...], rows_ref, bond), planes_ref)
    project(planes_ref, west, first_ref)
    mix(weights[...], first_ref, store_by_leg(mixed_ref, bond))
    kept_ref[...] = half(first_ref[...])

    def down(d, carry):
        block = leg_block(mixed_ref, d, bond)
        state_ref[row_block(d, size), :] = half(dot(block, east_ref[...], ((0,), (0,))))
        return carry

    loop(bond, down)


def up_kernel(
    env_ref, west_ref, east_ref, weights, kept_ref, state_ref,
    rows_ref, planes_ref, second_ref, mixed_ref,
):
    size = west_ref.shape[1]
    bond = west_ref.shape[0] // size
    west = joined(split_legs(west_ref[...], rows_ref, bond))
    stack(split_legs(env_ref[...], rows_ref, bond), planes_ref)
    pair_up(east_ref, planes_ref, True, second_ref)
    mix(weights[...], second_ref, store_natural(mixed_ref))
    kept_ref[...] = half(second_ref[...])

    def up(u, carry):
        low = joined(
            [
                half(flat(mixed_ref)[pl.ds(u * bond + k, size, stride=bond * bond), :])
                for k in range(bond)
            ]
        )
        state_ref[row_block(u, size), :] = half(dot(west, low, ((1,), (1,))))
        return carry

    loop(bond, up)


def upper_gradient(state_ref, east_ref, kept_ref, out_ref, volume_ref):
    pair_up(east_ref, state_ref, True, volume_ref)
    overlap(kept_ref, volume_ref, out_ref)


def lower_gradient(state_ref, west_ref, kept_ref, out_ref, rows_ref, volume_ref):
    bond = west_ref.shape[0] // west_ref.shape[1]
    project(state_ref, joined(split_legs(west_ref[...], rows_ref, bond)), volume_ref)
    overlap(volume_ref, kept_ref, out_ref)


def overlap(part_ref, key_ref, out_ref):
    outer, inner, lane = part_ref.shape
    group = 8

    def gather(ref, i):
        rows = flat(ref)
        return joined(
            [
                half(rows[pl.ds(pl.multiple_of((i * group + j) * inner, inner), inner), :])
                for j in range(group)
            ]
        )

    def step(i, total):
        return total + dot(gather(part_ref, i), gather(key_ref, i), ((1,), (1,)))

    out_ref[...] = lax.fori_loop(
        0, outer // group, step, jnp.zeros((inner, inner), jnp.float32)
    )


def upper_end_kernel(
    left_bulk, right_bulk, basis_ref, left_out, right_out, rows_ref
):
    for bulk, basis, out in (
        (left_bulk, basis_ref.at[: basis_ref.shape[0] // 2], left_out),
        (right_bulk, basis_ref.at[basis_ref.shape[0] // 2 :], right_out),
    ):
        bond, length, size = bulk.shape

        def step(i, total, bulk=bulk, basis=basis):
            rows = row_block(i, size)
            block = dot(
                joined([bulk[d, rows, :] for d in range(bond)]), basis[...], ((1,), (0,))
            )
            rows_ref[rows, :] = block
            return total + jnp.sum(block * block, axis=0, keepdims=True)

        scaled_out(loop(length // size, step, jnp.zeros((1, size))), rows_ref, out)


def scaled_out(total, rows_ref, out):
    mean = jnp.sum(total, keepdims=True) * (1.0 / (rows_ref.shape[0] * rows_ref.shape[1]))
    out[...] = half(rows_ref[...] * lax.rsqrt(mean + 1e-06))


def lower_end_kernel(
    left_bulk, right_bulk, basis_ref, left_out, right_out, rows_ref
):
    for bulk, basis, out in (
        (left_bulk, basis_ref.at[: basis_ref.shape[0] // 2], left_out),
        (right_bulk, basis_ref.at[basis_ref.shape[0] // 2 :], right_out),
    ):
        bond, length, size = bulk.shape
        flipped = basis[...].T

        def step(o, total, bulk=bulk, flipped=flipped):
            block = dot(flipped, bulk[o], ((1,), (0,)))
            rows_ref[pl.ds(o, size, stride=bond), :] = block
            return total + jnp.sum(block * block, axis=0, keepdims=True)

        scaled_out(loop(bond, step, jnp.zeros((1, size))), rows_ref, out)


def run(kernel, outs, scratch, flops, *args):
    in_vmem = pl.BlockSpec(memory_space=pltpu.VMEM)
    return pl.pallas_call(
        kernel,
        out_shape=tuple(jax.ShapeDtypeStruct(shape, kind) for shape, kind in outs),
        in_specs=[in_vmem] * len(args),
        out_specs=(in_vmem,) * len(outs),
        scratch_shapes=[pltpu.VMEM(shape, kind) for shape, kind in scratch],
        compiler_params=pltpu.CompilerParams(vmem_limit_bytes=48 * 1024 * 1024),
        cost_estimate=pl.CostEstimate(
            flops=flops, bytes_accessed=2_000_000, transcendentals=0
        ),
    )(*args)


def local(left_bounds, right_bounds, site_tensors, configuration, top_env, bottom_env, sketch):
    chi = left_bounds.shape[2]
    bond = left_bounds.shape[3]
    phys = site_tensors.shape[2]
    tall = (chi * bond, chi)
    wide = (bond, chi * bond, chi)
    double = (2 * chi * bond, chi)
    square = (bond * bond, bond * bond)
    volume = (chi, bond * bond, chi)
    row = lax.axis_index("row")
    leading = row == 0
    western = shift(left_bounds.reshape(tall), "col", 1)
    eastern = shift(right_bounds.reshape(tall), "col", -1)
    selection = (
        lax.broadcasted_iota(jnp.int32, (1, 1, phys, 1), 2) == configuration[:, :, None, None]
    )
    selected = jnp.sum(jnp.where(selection, site_tensors, jnp.zeros_like(site_tensors)), axis=2)
    core = selected.reshape(bond, bond, bond, bond)
    env = jnp.where(leading, top_env[0], bottom_env[0]).reshape(tall)
    base_left, base_right = run(
        edge_kernel,
        [(tall, BF16)] * 2,
        [(tall, F32), (tall, BF16), (tall, BF16)],
        10_000_000_000,
        env,
    )
    left_mix, right_mix = (
        jnp.where(leading, core.transpose(above), core.transpose(below)).reshape(square)
        for above, below in (((3, 2, 1, 0), (1, 2, 3, 0)), ((3, 0, 1, 2), (1, 0, 3, 2)))
    )

    def first_pass(kernel, weights):
        return lambda: run(
            kernel,
            [(volume, BF16), (tall, BF16)],
            [(tall, F32), (tall, BF16), (volume, F32), (volume, F32)],
            10_000_000_000,
            env,
            western,
            eastern,
            weights,
        )

    kept, state = lax.cond(
        leading, first_pass(down_kernel, left_mix), first_pass(up_kernel, right_mix)
    )
    received = lax.ppermute(state, "row", [(0, 1), (1, 0)])

    def upper():
        return run(
            upper_kernel,
            [(double, BF16)] + [(wide, BF16)] * 2,
            [(tall, F32), (volume, F32), (volume, F32), (tall, F32), (tall, F32)],
            10_000_000_000,
            base_left,
            base_right,
            western,
            eastern,
            left_mix,
            right_mix,
            sketch,
        )

    def lower():
        bulk_left, bulk_right = run(
            lower_kernel,
            [(wide, BF16)] * 2,
            [(volume, F32)] * 2,
            10_000_000_000,
            base_left,
            base_right,
            western,
            eastern,
            left_mix,
            right_mix,
        )
        return jnp.zeros(double, BF16), bulk_left, bulk_right

    following, bulk_left, bulk_right = lax.cond(leading, upper, lower)

    def lower_part():
        (result,) = run(
            lower_gradient,
            [(square, F32)],
            [(tall, F32), (volume, F32)],
            1_000_000_000,
            received,
            western,
            kept,
        )
        return result

    grad_lower = lax.cond(leading, lambda: jnp.zeros(square, F32), lower_part)
    grad_lower, following = lax.optimization_barrier((grad_lower, following))
    sent = lax.ppermute(following, "row", [(0, 1)])

    def end(kernel, basis):
        return run(
            kernel, [(tall, BF16)] * 2, [(tall, F32)], 1_000_000_000, bulk_left, bulk_right, basis
        )

    def upper_end():
        (result,) = run(
            upper_gradient,
            [(square, F32)],
            [(volume, F32)],
            1_000_000_000,
            received,
            eastern,
            kept,
        )
        return (result, *end(upper_end_kernel, following))

    def lower_end():
        return (grad_lower, *end(lower_end_kernel, sent))

    gradient, left_new, right_new = lax.cond(leading, upper_end, lower_end)
    gradient = gradient.reshape(bond, bond, bond, bond)
    gradient = gradient.transpose(1, 0, 3, 2).reshape(1, 1, 1, bond**4)
    gradient = jnp.where(selection, gradient * (bond / chi), 0.0)
    return (
        gradient,
        left_new.reshape(left_bounds.shape),
        right_new.reshape(right_bounds.shape),
    )


def solution(mesh):
    return jax.shard_map(
        local,
        mesh=mesh,
        in_specs=(
            P(("grp", "row"), "col", None, None, None),
            P(("grp", "row"), "col", None, None, None),
            P(("grp", "row"), "col", None, None),
            P(("grp", "row"), "col"),
            P(("grp", "col"), None, None, None),
            P(("grp", "col"), None, None, None),
            P(),
        ),
        out_specs=(
            P(("grp", "row"), "col", None, None),
            P(("grp", "row"), "col", None, None, None),
            P(("grp", "row"), "col", None, None, None),
        ),
        check_vma=False,
    )
```

time: 108 us -> 81.4 us (0.75)
  Pallas kernels: 82.9 us -> 58.9 us
  starting transfers between devices: 18.8 us -> 7.42 us
  waiting for transfers between devices: 0.02 us -> 9.23 us
    pallas_call x3 -> x5, Pallas kernels: 82.9 us -> 58.9 us  [run(): pl.pallas_call(kernel, out_shape=tuple((jax.ShapeDtypeStruct(shape, kind)...]
    ppermute x6 -> x2, starting transfers between devices: 15.4 us -> 1.33 us  [the longest x1 1.32 us: local(): sent = lax.ppermute(following, 'row', [(0, 1)])]
    ppermute x2, waiting for transfers between devices: 0.01 us -> 7.74 us  [shift(): lax.ppermute(value, axis, [(i, (i + distance) % count) for i in range(cou...]
    ppermute x2, starting transfers between devices: 3.37 us -> 6.09 us  [shift(): lax.ppermute(value, axis, [(i, (i + distance) % count) for i in range(cou...]
    ppermute x6 -> x2, waiting for transfers between devices: 0.02 us -> 1.49 us  [the longest x1 1.49 us: local(): sent = lax.ppermute(following, 'row', [(0, 1)])]
  transfers between devices with their start and end apart: 8 -> 4, of which waited for: 0 -> 3; matrix products, arithmetic and copies ran while one was open for 3% -> 2% of each run, Pallas kernels for 26% -> 52%
where the time goes in v1:
time: 81.4 us; the launch traced here: 81.1 us
  Pallas kernels  58.9 us (72%)
  waiting for transfers between devices  9.23 us (11%)
  starting transfers between devices  7.42 us (9%)
  local copies, waits for them, and re-layouts  2.27 us (3%)
  other arithmetic  1.66 us (2%)
  between operations  1.42 us (2%)
    pallas_call x5, Pallas kernels, run(): pl.pallas_call(kernel, out_shape=tuple((jax.ShapeDtypeStruct(shape, kind)...  58.9 us
    ppermute x2, waiting for transfers between devices, shift(): lax.ppermute(value, axis, [(i, (i + distance) % count) for i in range(cou...  7.74 us
    ppermute x2, starting transfers between devices, shift(): lax.ppermute(value, axis, [(i, (i + distance) % count) for i in range(cou...  6.09 us
  transfers between devices with their start and end apart: 4, of which 3 were waited for; matrix products, arithmetic and copies ran while one was open for 2% of the time, Pallas kernels for 52%

profile of v1, /device:TPU:0, one launch (start us, length us, event | category | flops | bytes accessed | tf_op | source)
XLA Modules:
  0.0 81.1 jit_solution(17388734685677464573)
XLA Ops:
  0.7 3.0 %collective-permute-start = (bf16[1024,128]{1,0:T(8,128)(2,1)}, bf16[1024,128]{1,0:T(8,128)(2,1)S(1)}, u32[]{:S(2)}, u32[]{:S(2)}) collective-permute-start(bf16[1024,128]{1,0:T(8,128)(2,1)} %bitcast.24), channel_id=1, source_target_pairs={{0,2},{2,4},{4,6},{6,8},{8,10},{10,12},{12,14},{14,0},{1,3},{3,5},... | collective-permute-start | bytes 786440 | tf_op jit(solution)/shard_map/ppermute | solution.py:14
  3.6 3.1 %collective-permute-start.1 = (bf16[1024,128]{1,0:T(8,128)(2,1)}, bf16[1024,128]{1,0:T(8,128)(2,1)S(1)}, u32[]{:S(2)}, u32[]{:S(2)}) collective-permute-start(bf16[1024,128]{1,0:T(8,128)(2,1)} %bitcast.25), channel_id=1, source_target_pairs={{0,14},{2,0},{4,2},{6,4},{8,6},{10,8},{12,10},{14,12},{1,15},{3,1}... | collective-permute-start | bytes 786440 | tf_op jit(solution)/shard_map/ppermute | solution.py:14
  7.4 0.8 %fusion = bf16[4096]{0:T(1024)(128)(2,1)S(1)} fusion(bf16[1,1,2,4096]{3,2,1,0:T(2,128)(2,1)} %param.17, pred[2]{0:T(512)(128)(4,1)S(1)} %iota_compare_fusion), kind=kLoop, calls=%fused_computation.6 | loop fusion | flops 12288 | bytes 24578 | tf_op jit(solution)/shard_map/reduce_sum | solution.py:431
  8.2 0.2 reshape.105
  8.4 0.2 copy.22
  8.6 0.2 copy.19
  9.0 0.1 reshape.106
  9.3 0.1 reshape.107
  9.5 5.6 %collective-permute-done = bf16[1024,128]{1,0:T(8,128)(2,1)S(1)} collective-permute-done((bf16[1024,128]{1,0:T(8,128)(2,1)}, bf16[1024,128]{1,0:T(8,128)(2,1)S(1)}, u32[]{:S(2)}, u32[]{:S(2)}) %collective-permute-start) | collective-permute-done | bytes 262176 | tf_op jit(solution)/shard_map/ppermute | solution.py:14
  15.1 2.1 %collective-permute-done.1 = bf16[1024,128]{1,0:T(8,128)(2,1)S(1)} collective-permute-done((bf16[1024,128]{1,0:T(8,128)(2,1)}, bf16[1024,128]{1,0:T(8,128)(2,1)S(1)}, u32[]{:S(2)}, u32[]{:S(2)}) %collective-permute-start.1) | collective-permute-done | bytes 262176 | tf_op jit(solution)/shard_map/ppermute | solution.py:14
  17.2 7.9 %conditional.5 = ((bf16[128,64,128]{2,1,0:T(8,128)(2,1)}, bf16[1024,128]{1,0:T(8,128)(2,1)})) conditional(s32[]{:T(128)} %convert_element_type.2, (bf16[1024,128]{1,0:T(8,128)(2,1)S(1)}, bf16[1024,128]{1,0:T(8,128)(2,1)S(1)}, bf16[1024,128]{1,0:T(8,128)(2,1)S(1)}, bf16[64,64]{1,0:T(8,128)(2,1)S(1)}) %tuple.38, (bf16[1024,128]{1,0:T(8,128)(2,1)S(1)}, ...), branch_computations={%region_3.4_spmd, %region_4.5_spmd} | conditional | flops 10000000000 | bytes 2000008 | solution.py:458
  17.2 7.8 %branch_1_fun.5 = (bf16[128,64,128]{2,1,0:T(8,128)(2,1)}, bf16[1024,128]{1,0:T(8,128)(2,1)}) custom-call(bf16[1024,128]{1,0:T(8,128)(2,1)S(1)} %get-tuple-element.90.env_ref, bf16[1024,128]{1,0:T(8,128)(2,1)S(1)} %get-tuple-element.91.west_ref, bf16[1024,128]{1,0:T(8,128)(2,1)S(1)} %get-tuple-element.92.east_ref, bf16[64,64]{1,0:T(8,128)(2,1)S(1)} %get-tuple-element.93.weights), custom_call_target="tpu_custom_call" | custom-call | flops 10000000000 | bytes 2000000 | tf_op jit(solution)/shard_map/cond/branch_1_fun/pallas_call | solution.py:402
  25.1 12.6 %shard_map.95 = (bf16[1024,128]{1,0:T(8,128)(2,1)S(1)}, bf16[1024,128]{1,0:T(8,128)(2,1)S(1)}) custom-call(bf16[1024,128]{1,0:T(8,128)(2,1)S(1)} %select_bitcast_fusion.env_ref), custom_call_target="tpu_custom_call" | custom-call | flops 10000000000 | bytes 2000000 | tf_op jit(solution)/shard_map/pallas_call | solution.py:402
  37.7 30.2 %conditional.4 = ((bf16[2048,128]{1,0:T(8,128)(2,1)S(1)}, bf16[8,1024,128]{2,1,0:T(8,128)(2,1)S(1)}, bf16[8,1024,128]{2,1,0:T(8,128)(2,1)})) conditional(s32[]{:T(128)} %convert_element_type.2, (bf16[1024,128]{1,0:T(8,128)(2,1)S(1)}, bf16[1024,128]{1,0:T(8,128)(2,1)S(1)}, bf16[1024,128]{1,0:T(8,128)(2,1)S(1)}, bf16[1024,128]{1,0:T(8,128)(2,1)S(1)}, ...), branch_computations={%region_1.2_spmd, %region_2.3_spmd} | conditional | flops 10000000000 | bytes 4097216 | solution.py:493
  38.0 0.7 copy-done.4
  38.8 29.2 %branch_1_fun.4 = (bf16[2048,128]{1,0:T(8,128)(2,1)S(1)}, bf16[8,1024,128]{2,1,0:T(8,128)(2,1)S(1)}, bf16[8,1024,128]{2,1,0:T(8,128)(2,1)}) custom-call(bf16[1024,128]{1,0:T(8,128)(2,1)} %copy-done.4, bf16[1024,128]{1,0:T(8,128)(2,1)} %copy-done.5, bf16[1024,128]{1,0:T(8,128)(2,1)S(1)} %get-tuple-element.81.west_ref, ...), custom_call_target="tpu_custom_call" | custom-call | flops 10000000000 | bytes 2000000 | tf_op jit(solution)/shard_map/cond/branch_1_fun/pallas_call | solution.py:402
  68.0 1.3 %collective-permute-start.3 = (bf16[2048,128]{1,0:T(8,128)(2,1)S(1)}, bf16[2048,128]{1,0:T(8,128)(2,1)S(1)}, u32[]{:S(2)}, u32[]{:S(2)}) collective-permute-start(bf16[2048,128]{1,0:T(8,128)(2,1)S(1)} %get-tuple-element.133), channel_id=1, source_target_pairs={{0,1},{2,3},{4,5},{6,7},{8,9},{10,11},{12,13},{14,15},{16,17},{18,... | collective-permute-start | bytes 1572872 | tf_op jit(solution)/shard_map/ppermute | solution.py:509
  69.3 1.5 %collective-permute-done.3 = bf16[2048,128]{1,0:T(8,128)(2,1)S(1)} collective-permute-done((bf16[2048,128]{1,0:T(8,128)(2,1)S(1)}, bf16[2048,128]{1,0:T(8,128)(2,1)S(1)}, u32[]{:S(2)}, u32[]{:S(2)}) %collective-permute-start.3) | collective-permute-done | bytes 524320 | tf_op jit(solution)/shard_map/ppermute | solution.py:509
  70.8 9.2 %conditional.7 = (f32[64,64]{1,0:T(8,128)S(1)}, bf16[1024,128]{1,0:T(8,128)(2,1)}, bf16[1024,128]{1,0:T(8,128)(2,1)}) conditional(s32[]{:T(128)} %convert_element_type.2, (bf16[8,1024,128]{2,1,0:T(8,128)(2,1)S(1)}, bf16[8,1024,128]{2,1,0:T(8,128)(2,1)}, bf16[2048,128]{1,0:T(8,128)(2,1)S(1)}, f32[64,64]{1,0:T(8,128)S(1)}) %tuple.43, ...), branch_computations={%region_7.8_spmd, %region_8.9_spmd} | conditional | flops 2000000000 | bytes 12388660 | solution.py:531
  70.8 5.8 %branch_1_fun.6 = f32[64,64]{1,0:T(8,128)S(1)} custom-call(bf16[1024,128]{1,0:T(8,128)(2,1)S(1)} %get-tuple-element.103.state_ref, bf16[1024,128]{1,0:T(8,128)(2,1)S(1)} %get-tuple-element.104.east_ref, bf16[128,64,128]{2,1,0:T(8,128)(2,1)} %get-tuple-element.105.kept_ref), custom_call_target="tpu_custom_call" | custom-call | flops 1000000000 | bytes 2000000 | tf_op jit(solution)/shard_map/cond/branch_1_fun/pallas_call | solution.py:402
  76.6 3.4 %branch_1_fun.7 = (bf16[1024,128]{1,0:T(8,128)(2,1)}, bf16[1024,128]{1,0:T(8,128)(2,1)}) custom-call(bf16[8,1024,128]{2,1,0:T(8,128)(2,1)S(1)} %get-tuple-element.106.left_bulk, bf16[8,1024,128]{2,1,0:T(8,128)(2,1)S(1)} %copy-done, bf16[2048,128]{1,0:T(8,128)(2,1)S(1)} %get-tuple-element.108.basis_ref), custom_call_target="tpu_custom_call" | custom-call | flops 1000000000 | bytes 2000000 | tf_op jit(solution)/shard_map/cond/branch_1_fun/pallas_call | solution.py:402
  80.1 0.1 copy.24
  80.3 0.1 mul.24
  80.4 0.7 broadcast_select_fusion
  (22 shorter events, 0.7 us)
Async XLA Ops:
  0.6 8.8 %copy-start.1 = (bf16[1,128,8,128]{3,2,1,0:T(8,128)(2,1)S(1)}, bf16[1,128,8,128]{3,2,1,0:T(8,128)(2,1)}, u32[]{:S(2)}) copy-start(bf16[1,128,8,128]{3,2,1,0:T(8,128)(2,1)} %param.19) | copy-start | bytes 786436
  0.6 8.8 %copy-start.2 = (bf16[1,128,8,128]{3,2,1,0:T(8,128)(2,1)S(1)}, bf16[1,128,8,128]{3,2,1,0:T(8,128)(2,1)}, u32[]{:S(2)}) copy-start(bf16[1,128,8,128]{3,2,1,0:T(8,128)(2,1)} %param.20) | copy-start | bytes 786436
  0.7 14.5 %collective-permute-start = (bf16[1024,128]{1,0:T(8,128)(2,1)}, bf16[1024,128]{1,0:T(8,128)(2,1)S(1)}, u32[]{:S(2)}, u32[]{:S(2)}) collective-permute-start(bf16[1024,128]{1,0:T(8,128)(2,1)} %bitcast.24), channel_id=1, source_target_pairs={{0,2},{2,4},{4,6},{6,8},{8,10},{10,12},{12,14},{14,0},{1,3},{3,5},... | collective-permute-start | bytes 786440 | tf_op jit(solution)/shard_map/ppermute | solution.py:14
  3.6 13.6 %collective-permute-start.1 = (bf16[1024,128]{1,0:T(8,128)(2,1)}, bf16[1024,128]{1,0:T(8,128)(2,1)S(1)}, u32[]{:S(2)}, u32[]{:S(2)}) collective-permute-start(bf16[1024,128]{1,0:T(8,128)(2,1)} %bitcast.25), channel_id=1, source_target_pairs={{0,14},{2,0},{4,2},{6,4},{8,6},{10,8},{12,10},{14,12},{1,15},{3,1}... | collective-permute-start | bytes 786440 | tf_op jit(solution)/shard_map/ppermute | solution.py:14
  25.1 12.6 %copy-start.3 = (bf16[1024,128]{1,0:T(8,128)(2,1)S(1)}, bf16[1024,128]{1,0:T(8,128)(2,1)}, u32[]{:S(2)}) copy-start(bf16[1024,128]{1,0:T(8,128)(2,1)} %param.21) | copy-start | bytes 786436
  25.1 42.9 %collective-permute-start.2 = (bf16[1024,128]{1,0:T(8,128)(2,1)}, bf16[1024,128]{1,0:T(8,128)(2,1)S(1)}, u32[]{:S(2)}, u32[]{:S(2)}) collective-permute-start(bf16[1024,128]{1,0:T(8,128)(2,1)} %get-tuple-element.130), channel_id=1, source_target_pairs={{0,1},{1,0},{2,3},{3,2},{4,5},{5,4},{6,7},{7,6},{8,9},{9,8},{10,11... | collective-permute-start | bytes 786440 | tf_op jit(solution)/shard_map/ppermute | solution.py:461
  37.9 0.7 copy-start.4
  38.0 0.8 copy-start.5
  68.0 2.8 %collective-permute-start.3 = (bf16[2048,128]{1,0:T(8,128)(2,1)S(1)}, bf16[2048,128]{1,0:T(8,128)(2,1)S(1)}, u32[]{:S(2)}, u32[]{:S(2)}) collective-permute-start(bf16[2048,128]{1,0:T(8,128)(2,1)S(1)} %get-tuple-element.133), channel_id=1, source_target_pairs={{0,1},{2,3},{4,5},{6,7},{8,9},{10,11},{12,13},{14,15},{16,17},{18,... | collective-permute-start | bytes 1572872 | tf_op jit(solution)/shard_map/ppermute | solution.py:509
  70.8 5.8 %copy-start = (bf16[8,1024,128]{2,1,0:T(8,128)(2,1)S(1)}, bf16[8,1024,128]{2,1,0:T(8,128)(2,1)}, u32[]{:S(2)}) copy-start(bf16[8,1024,128]{2,1,0:T(8,128)(2,1)} %get-tuple-element.107.right_bulk) | copy-start | bytes 6291460 | tf_op jit(solution)/shard_map/cond

commit v2 on v1

--- a/solution.py
+++ b/solution.py
@@ -63,7 +63,7 @@
     return [jnp.concatenate(blocks, axis=0) for blocks in found]
 
 
-def loop(count, step, start=0, unroll=2):
+def loop(count, step, start=0, unroll=4):
     def several(i, carry):
         for j in range(unroll):
             carry = step(i * unroll + j, carry)
@@ -84,7 +84,7 @@
         return total + dot(block, block, ((0,), (0,)), precision)
 
     start = jnp.zeros((size, size), jnp.float32)
-    return loop(source.shape[0] // size, step, start)
+    return loop(source.shape[0] // size, step, start, 8)
 
 
 def apply_transposed(source, inverse, out):
@@ -110,7 +110,7 @@
             out[row_block(i, size), :] = total.astype(jnp.bfloat16)
             return carry
 
-    loop(source.shape[0] // size, step)
+    loop(source.shape[0] // size, step, unroll=8)
 
 
 BF16 = jnp.bfloat16
@@ -371,7 +371,7 @@
             rows_ref[rows, :] = block
             return total + jnp.sum(block * block, axis=0, keepdims=True)
 
-        scaled_out(loop(length // size, step, jnp.zeros((1, size))), rows_ref, out)
+        scaled_out(loop(length // size, step, jnp.zeros((1, size)), 8), rows_ref, out)
 
 
 def scaled_out(total, rows_ref, out):
@@ -394,7 +394,7 @@
             rows_ref[pl.ds(o, size, stride=bond), :] = block
             return total + jnp.sum(block * block, axis=0, keepdims=True)
 
-        scaled_out(loop(bond, step, jnp.zeros((1, size))), rows_ref, out)
+        scaled_out(loop(bond, step, jnp.zeros((1, size)), 8), rows_ref, out)
 
 
 def run(kernel, outs, scratch, flops, *args):
@@ -438,6 +438,7 @@
         10_000_000_000,
         env,
     )
+    env, base_left = lax.optimization_barrier((env, base_left))
     left_mix, right_mix = (
         jnp.where(leading, core.transpose(above), core.transpose(below)).reshape(square)
         for above, below in (((3, 2, 1, 0), (1, 2, 3, 0)), ((3, 0, 1, 2), (1, 0, 3, 2)))

time: 81.4 us -> 63.7 us (0.78)
  Pallas kernels: 58.9 us -> 48.6 us
  waiting for transfers between devices: 9.23 us -> 1.49 us
    pallas_call x5, Pallas kernels: 58.9 us -> 48.6 us  [run(): pl.pallas_call(kernel, out_shape=tuple((jax.ShapeDtypeStruct(shape, kind)...]
    ppermute x2, waiting for transfers between devices: 7.74 us -> 0.01 us  [shift(): lax.ppermute(value, axis, [(i, (i + distance) % count) for i in range(cou...]
    select_n x1, other arithmetic: 0.03 us -> 0.99 us  [local(): env = jnp.where(leading, top_env[0], bottom_env[0]).reshape(tall)]
  transfers between devices with their start and end apart: 4 -> 4, of which waited for: 3 -> 1; matrix products, arithmetic and copies ran while one was open for 2% -> 4% of each run, Pallas kernels for 52% -> 54%
where the time goes in v2:
time: 63.7 us; the launch traced here: 63.5 us
  Pallas kernels  48.6 us (76%)
  starting transfers between devices  7.42 us (12%)
  local copies, waits for them, and re-layouts  2.27 us (4%)
  other arithmetic  1.91 us (3%)
  waiting for transfers between devices  1.49 us (2%)
  between operations  1.42 us (2%)
    pallas_call x5, Pallas kernels, run(): pl.pallas_call(kernel, out_shape=tuple((jax.ShapeDtypeStruct(shape, kind)...  48.6 us
    ppermute x2, starting transfers between devices, shift(): lax.ppermute(value, axis, [(i, (i + distance) % count) for i in range(cou...  6.09 us
    ppermute x1, waiting for transfers between devices, local(): sent = lax.ppermute(following, 'row', [(0, 1)])  1.49 us
    ppermute x1, starting transfers between devices, local(): sent = lax.ppermute(following, 'row', [(0, 1)])  1.32 us
  transfers between devices with their start and end apart: 4, of which 1 were waited for; matrix products, arithmetic and copies ran while one was open for 4% of the time, Pallas kernels for 54%

profile of v2, /device:TPU:0, one launch (start us, length us, event | category | flops | bytes accessed | tf_op | source)
XLA Modules:
  0.0 63.5 jit_solution(5859040802248843629)
XLA Ops:
  0.6 3.0 %collective-permute-start = (bf16[1024,128]{1,0:T(8,128)(2,1)}, bf16[1024,128]{1,0:T(8,128)(2,1)S(1)}, u32[]{:S(2)}, u32[]{:S(2)}) collective-permute-start(bf16[1024,128]{1,0:T(8,128)(2,1)} %bitcast.24), channel_id=1, source_target_pairs={{0,2},{2,4},{4,6},{6,8},{8,10},{10,12},{12,14},{14,0},{1,3},{3,5},... | collective-permute-start | bytes 786440 | tf_op jit(solution)/shard_map/ppermute | solution.py:14
  3.6 3.1 %collective-permute-start.1 = (bf16[1024,128]{1,0:T(8,128)(2,1)}, bf16[1024,128]{1,0:T(8,128)(2,1)S(1)}, u32[]{:S(2)}, u32[]{:S(2)}) collective-permute-start(bf16[1024,128]{1,0:T(8,128)(2,1)} %bitcast.25), channel_id=1, source_target_pairs={{0,14},{2,0},{4,2},{6,4},{8,6},{10,8},{12,10},{14,12},{1,15},{3,1}... | collective-permute-start | bytes 786440 | tf_op jit(solution)/shard_map/ppermute | solution.py:14
  7.4 1.0 %select_bitcast_fusion.env_ref = bf16[1024,128]{1,0:T(8,128)(2,1)S(1)} fusion(bf16[1,128,8,128]{3,2,1,0:T(8,128)(2,1)} %param.19, bf16[1,128,8,128]{3,2,1,0:T(8,128)(2,1)} %param.20, pred[]{:T(512)S(6)} %eq.21), kind=kLoop, calls=%fused_computation | loop fusion | flops 131072 | bytes 786433 | tf_op jit(solution)/shard_map/jit(_where)/select_n | solution.py:433
  8.4 10.8 %shard_map.95 = (bf16[1024,128]{1,0:T(8,128)(2,1)S(1)}, bf16[1024,128]{1,0:T(8,128)(2,1)S(1)}) custom-call(bf16[1024,128]{1,0:T(8,128)(2,1)S(1)} %select_bitcast_fusion.env_ref), custom_call_target="tpu_custom_call" | custom-call | flops 10000000000 | bytes 2000000 | tf_op jit(solution)/shard_map/pallas_call | solution.py:402
  19.3 0.2 reshape.105
  19.5 0.2 copy.22
  19.6 0.2 copy.19
  19.9 0.1 copy.21
  20.1 0.1 reshape.106
  20.2 0.1 copy.23
  20.3 0.1 reshape.107
  20.5 6.6 %conditional.5 = ((bf16[128,64,128]{2,1,0:T(8,128)(2,1)}, bf16[1024,128]{1,0:T(8,128)(2,1)})) conditional(s32[]{:T(128)} %convert_element_type.2, (bf16[1024,128]{1,0:T(8,128)(2,1)S(1)}, bf16[1024,128]{1,0:T(8,128)(2,1)S(1)}, bf16[1024,128]{1,0:T(8,128)(2,1)S(1)}, bf16[64,64]{1,0:T(8,128)(2,1)S(1)}) %tuple.40, (bf16[1024,128]{1,0:T(8,128)(2,1)S(1)}, ...), branch_computations={%region_3.4_spmd, %region_4.5_spmd} | conditional | flops 10000000000 | bytes 2000008 | solution.py:459
  20.7 6.4 %branch_1_fun.5 = (bf16[128,64,128]{2,1,0:T(8,128)(2,1)}, bf16[1024,128]{1,0:T(8,128)(2,1)}) custom-call(bf16[1024,128]{1,0:T(8,128)(2,1)S(1)} %get-tuple-element.90.env_ref, bf16[1024,128]{1,0:T(8,128)(2,1)S(1)} %get-tuple-element.91.west_ref, bf16[1024,128]{1,0:T(8,128)(2,1)S(1)} %get-tuple-element.92.east_ref, bf16[64,64]{1,0:T(8,128)(2,1)S(1)} %get-tuple-element.93.weights), custom_call_target="tpu_custom_call" | custom-call | flops 10000000000 | bytes 2000000 | tf_op jit(solution)/shard_map/cond/branch_1_fun/pallas_call | solution.py:402
  27.1 24.7 %conditional.4 = ((bf16[2048,128]{1,0:T(8,128)(2,1)S(1)}, bf16[8,1024,128]{2,1,0:T(8,128)(2,1)S(1)}, bf16[8,1024,128]{2,1,0:T(8,128)(2,1)})) conditional(s32[]{:T(128)} %convert_element_type.2, (bf16[1024,128]{1,0:T(8,128)(2,1)S(1)}, bf16[1024,128]{1,0:T(8,128)(2,1)S(1)}, bf16[1024,128]{1,0:T(8,128)(2,1)S(1)}, bf16[1024,128]{1,0:T(8,128)(2,1)S(1)}, ...), branch_computations={%region_1.2_spmd, %region_2.3_spmd} | conditional | flops 10000000000 | bytes 4097216 | solution.py:494
  27.1 0.7 %copy-done.3 = bf16[1024,128]{1,0:T(8,128)(2,1)} copy-done((bf16[1024,128]{1,0:T(8,128)(2,1)}, bf16[1024,128]{1,0:T(8,128)(2,1)S(1)}, u32[]{:S(2)}) %copy-start.3) | copy-done | bytes 262168 | tf_op jit(solution)/shard_map/cond
  27.9 23.7 %branch_1_fun.4 = (bf16[2048,128]{1,0:T(8,128)(2,1)S(1)}, bf16[8,1024,128]{2,1,0:T(8,128)(2,1)S(1)}, bf16[8,1024,128]{2,1,0:T(8,128)(2,1)}) custom-call(bf16[1024,128]{1,0:T(8,128)(2,1)} %copy-done.3, bf16[1024,128]{1,0:T(8,128)(2,1)} %copy-done.4, bf16[1024,128]{1,0:T(8,128)(2,1)S(1)} %get-tuple-element.81.west_ref, ...), custom_call_target="tpu_custom_call" | custom-call | flops 10000000000 | bytes 2000000 | tf_op jit(solution)/shard_map/cond/branch_1_fun/pallas_call | solution.py:402
  51.8 1.3 %collective-permute-start.3 = (bf16[2048,128]{1,0:T(8,128)(2,1)S(1)}, bf16[2048,128]{1,0:T(8,128)(2,1)S(1)}, u32[]{:S(2)}, u32[]{:S(2)}) collective-permute-start(bf16[2048,128]{1,0:T(8,128)(2,1)S(1)} %get-tuple-element.137), channel_id=1, source_target_pairs={{0,1},{2,3},{4,5},{6,7},{8,9},{10,11},{12,13},{14,15},{16,17},{18,... | collective-permute-start | bytes 1572872 | tf_op jit(solution)/shard_map/ppermute | solution.py:510
  53.2 1.5 %collective-permute-done.3 = bf16[2048,128]{1,0:T(8,128)(2,1)S(1)} collective-permute-done((bf16[2048,128]{1,0:T(8,128)(2,1)S(1)}, bf16[2048,128]{1,0:T(8,128)(2,1)S(1)}, u32[]{:S(2)}, u32[]{:S(2)}) %collective-permute-start.3) | collective-permute-done | bytes 524320 | tf_op jit(solution)/shard_map/ppermute | solution.py:510
  54.7 7.8 %conditional.7 = (f32[64,64]{1,0:T(8,128)S(1)}, bf16[1024,128]{1,0:T(8,128)(2,1)}, bf16[1024,128]{1,0:T(8,128)(2,1)}) conditional(s32[]{:T(128)} %convert_element_type.2, (bf16[8,1024,128]{2,1,0:T(8,128)(2,1)S(1)}, bf16[8,1024,128]{2,1,0:T(8,128)(2,1)}, bf16[2048,128]{1,0:T(8,128)(2,1)S(1)}, f32[64,64]{1,0:T(8,128)S(1)}) %tuple.45, ...), branch_computations={%region_7.8_spmd, %region_8.9_spmd} | conditional | flops 2000000000 | bytes 12388660 | solution.py:532
  54.7 5.6 %branch_1_fun.6 = f32[64,64]{1,0:T(8,128)S(1)} custom-call(bf16[1024,128]{1,0:T(8,128)(2,1)} %get-tuple-element.103.state_ref, bf16[1024,128]{1,0:T(8,128)(2,1)S(1)} %get-tuple-element.104.east_ref, bf16[128,64,128]{2,1,0:T(8,128)(2,1)} %get-tuple-element.105.kept_ref), custom_call_target="tpu_custom_call" | custom-call | flops 1000000000 | bytes 2000000 | tf_op jit(solution)/shard_map/cond/branch_1_fun/pallas_call | solution.py:402
  60.2 2.2 %branch_1_fun.7 = (bf16[1024,128]{1,0:T(8,128)(2,1)}, bf16[1024,128]{1,0:T(8,128)(2,1)}) custom-call(bf16[8,1024,128]{2,1,0:T(8,128)(2,1)S(1)} %get-tuple-element.106.left_bulk, bf16[8,1024,128]{2,1,0:T(8,128)(2,1)S(1)} %copy-done, bf16[2048,128]{1,0:T(8,128)(2,1)S(1)} %get-tuple-element.108.basis_ref), custom_call_target="tpu_custom_call" | custom-call | flops 1000000000 | bytes 2000000 | tf_op jit(solution)/shard_map/cond/branch_1_fun/pallas_call | solution.py:402
  62.6 0.1 copy.24
  62.7 0.1 mul.24
  62.8 0.7 %broadcast_select_fusion = f32[1,1,2,4096]{3,2,1,0:T(2,128)} fusion(pred[2]{0:T(512)(128)(4,1)S(1)} %iota_compare_fusion, f32[4096]{0:T(1024)S(1)} %mul.24), kind=kLoop, calls=%fused_computation.3 | loop fusion | flops 8192 | bytes 49154 | tf_op jit(solution)/shard_map/jit(_where)/select_n | solution.py:535
  (20 shorter events, 0.5 us)
Async XLA Ops:
  0.6 19.8 %collective-permute-start = (bf16[1024,128]{1,0:T(8,128)(2,1)}, bf16[1024,128]{1,0:T(8,128)(2,1)S(1)}, u32[]{:S(2)}, u32[]{:S(2)}) collective-permute-start(bf16[1024,128]{1,0:T(8,128)(2,1)} %bitcast.24), channel_id=1, source_target_pairs={{0,2},{2,4},{4,6},{6,8},{8,10},{10,12},{12,14},{14,0},{1,3},{3,5},... | collective-permute-start | bytes 786440 | tf_op jit(solution)/shard_map/ppermute | solution.py:14
  3.6 16.9 %collective-permute-start.1 = (bf16[1024,128]{1,0:T(8,128)(2,1)}, bf16[1024,128]{1,0:T(8,128)(2,1)S(1)}, u32[]{:S(2)}, u32[]{:S(2)}) collective-permute-start(bf16[1024,128]{1,0:T(8,128)(2,1)} %bitcast.25), channel_id=1, source_target_pairs={{0,14},{2,0},{4,2},{6,4},{8,6},{10,8},{12,10},{14,12},{1,15},{3,1}... | collective-permute-start | bytes 786440 | tf_op jit(solution)/shard_map/ppermute | solution.py:14
  8.4 10.8 %copy-start.1 = (bf16[1,1,2,4096]{3,2,1,0:T(2,128)(2,1)S(1)}, bf16[1,1,2,4096]{3,2,1,0:T(2,128)(2,1)}, u32[]{:S(2)}) copy-start(bf16[1,1,2,4096]{3,2,1,0:T(2,128)(2,1)} %param.17) | copy-start | bytes 49156
  20.5 6.6 %copy-start.2 = (bf16[1024,128]{1,0:T(8,128)(2,1)S(1)}, bf16[1024,128]{1,0:T(8,128)(2,1)}, u32[]{:S(2)}) copy-start(bf16[1024,128]{1,0:T(8,128)(2,1)} %param.21) | copy-start | bytes 786436
  27.1 24.7 %collective-permute-start.2 = (bf16[1024,128]{1,0:T(8,128)(2,1)}, bf16[1024,128]{1,0:T(8,128)(2,1)}, u32[]{:S(2)}, u32[]{:S(2)}) collective-permute-start(bf16[1024,128]{1,0:T(8,128)(2,1)} %get-tuple-element.134), channel_id=1, source_target_pairs={{0,1},{1,0},{2,3},{3,2},{4,5},{5,4},{6,7},{7,6},{8,9},{9,8},{10,11... | collective-permute-start | bytes 786440 | tf_op jit(solution)/shard_map/ppermute | solution.py:462
  27.1 0.7 %copy-start.3 = (bf16[1024,128]{1,0:T(8,128)(2,1)}, bf16[1024,128]{1,0:T(8,128)(2,1)S(1)}, u32[]{:S(2)}) copy-start(bf16[1024,128]{1,0:T(8,128)(2,1)S(1)} %get-tuple-element.79.left_base) | copy-start | bytes 786436 | tf_op jit(solution)/shard_map/cond
  27.1 0.8 %copy-start.4 = (bf16[1024,128]{1,0:T(8,128)(2,1)}, bf16[1024,128]{1,0:T(8,128)(2,1)S(1)}, u32[]{:S(2)}) copy-start(bf16[1024,128]{1,0:T(8,128)(2,1)S(1)} %get-tuple-element.80.right_base) | copy-start | bytes 786436 | tf_op jit(solution)/shard_map/cond
  51.8 2.8 %collective-permute-start.3 = (bf16[2048,128]{1,0:T(8,128)(2,1)S(1)}, bf16[2048,128]{1,0:T(8,128)(2,1)S(1)}, u32[]{:S(2)}, u32[]{:S(2)}) collective-permute-start(bf16[2048,128]{1,0:T(8,128)(2,1)S(1)} %get-tuple-element.137), channel_id=1, source_target_pairs={{0,1},{2,3},{4,5},{6,7},{8,9},{10,11},{12,13},{14,15},{16,17},{18,... | collective-permute-start | bytes 1572872 | tf_op jit(solution)/shard_map/ppermute | solution.py:510
  54.7 5.6 %copy-start = (bf16[8,1024,128]{2,1,0:T(8,128)(2,1)S(1)}, bf16[8,1024,128]{2,1,0:T(8,128)(2,1)}, u32[]{:S(2)}) copy-start(bf16[8,1024,128]{2,1,0:T(8,128)(2,1)} %get-tuple-element.107.right_bulk) | copy-start | bytes 6291460 | tf_op jit(solution)/shard_map/cond
